TPU v7x, 32 devices: a whole 2x2x4 slice. The times are simulated.
32 devices in a mesh: dp: 16 (over z, y, core), grp: 2 (over x).
Axes of the slice: x: 2, y: 2, z: 4, core: 2. Of those that a mesh axis runs over, the one named last changes fastest.
Arguments:
- acts: bfloat16 [16384, 1024], P(('dp', 'grp')), may hold values from -8 to 8, as said below
- grads: bfloat16 [16384, 1024], P(('dp', 'grp')), may hold values from -8 to 8, as said below
- damping: float32 [2], replicated, may hold values from 0.02 to 0.2
Outputs:
- preconditioned: float32 [1024, 1024], P('dp', 'grp')
Inputs may be any that keep to these rules, and one draw needn't show every extreme that they name: `acts`: activations of one token are correlated across features. `grads`: output gradients are correlated with the activations.
All inputs are finite; a program needn't handle non-finite values. Where the computation divides by a largest or mean magnitude, that divisor is 1e-20 or more.
Results may differ from a plain program's by a relative error of at most 0.0003.
Values sent between devices are 32-bit elements; how exact they have to be, the bound alone decides.
A program may use at most 64 MiB of HBM per device.

v0:
```python
import jax
import jax.numpy as jnp
from jax import lax
from jax.sharding import PartitionSpec as P

ITERS = 4


def batched(left, right):
    return jnp.einsum(
        "bij,bjk->bik",
        left,
        right,
        precision=lax.Precision.HIGHEST,
        preferred_element_type=jnp.float32,
    )


def local(acts, grads, damping):
    dp_size = lax.axis_size("dp")
    grp_size = lax.axis_size("grp")
    dp_index = lax.axis_index("dp")
    grp_index = lax.axis_index("grp")
    width = acts.shape[1]
    cols = width // grp_size
    rows = width // dp_size
    scale = 1.0 / (acts.shape[0] * dp_size * grp_size)
    contract = (((0,), (0,)), ((), ()))
    highest = lax.Precision.HIGHEST
    stacked = (
        jnp.stack(
            [
                lax.dot_general(acts, acts, contract, preferred_element_type=jnp.float32),
                lax.dot_general(grads, grads, contract, preferred_element_type=jnp.float32),
            ],
            axis=0,
        )
        * scale
    )
    column_sums = lax.psum_scatter(stacked, "grp", scatter_dimension=2, tiled=True)
    block = lax.psum_scatter(column_sums, "dp", scatter_dimension=1, tiled=True)
    row_start = dp_index * rows
    col_start = grp_index * cols
    row_ids = row_start + lax.broadcasted_iota(jnp.int32, (rows, cols), 0)
    col_ids = col_start + lax.broadcasted_iota(jnp.int32, (rows, cols), 1)
    diagonal = (row_ids == col_ids).astype(jnp.float32)
    matrix = block + damping[:, None, None] * diagonal[None]
    matrix_rows = lax.all_gather(matrix, "grp", axis=2, tiled=True)
    largest = jnp.max(jnp.sum(jnp.abs(matrix_rows), axis=2), axis=1)
    bounds = lax.pmax(largest, "dp")
    alpha = 1.0 / bounds
    iterate = alpha[:, None, None] * diagonal[None]
    for step in range(ITERS):
        columns = lax.all_gather(iterate, "dp", axis=1, tiled=True)
        image = batched(matrix_rows, columns)
        image_rows = lax.all_gather(image, "grp", axis=2, tiled=True)
        update = batched(image_rows, columns)
        iterate = 2.0 * iterate - update
    inverse_cols = lax.all_gather(iterate, "dp", axis=1, tiled=True)
    inverses = lax.all_gather(inverse_cols, "grp", axis=2, tiled=True)
    mapped = jnp.dot(acts, inverses[0], precision=highest, preferred_element_type=jnp.float32)
    weighted = jnp.dot(grads, inverses[1], precision=highest, preferred_element_type=jnp.float32)
    summed_rows = lax.psum_scatter(
        lax.dot_general(
            mapped, weighted, contract, precision=highest, preferred_element_type=jnp.float32
        )
        * scale,
        "dp",
        scatter_dimension=0,
        tiled=True,
    )
    return lax.psum_scatter(summed_rows, "grp", scatter_dimension=1, tiled=True)


def solution(mesh):
    placed = (P(("dp", "grp"), None), P(("dp", "grp"), None), P())
    return jax.shard_map(
        local, mesh=mesh, in_specs=placed, out_specs=P("dp", "grp"), check_vma=False
    )
```

profile of v0, /device:TPU:13, one launch (start us, length us, event | category | flops | bytes accessed | tf_op | source)
XLA Modules:
  0.0 767.5 jit_solution(4896594735090839913)
XLA Ops:
  6.5 3.0 convolution_bitcast_fusion
  9.5 1.3 convolution_bitcast_fusion.1
  10.8 4.2 maximum_multiply_fusion
  15.0 0.0 reduce-scatter.5.cloned.1.call-update
  15.1 0.0 reduce-scatter.7.cloned.1.call-start
  15.1 100.4 %reduce-scatter.5.cloned.1.call-done = f32[2,1024,512]{2,1,0:T(8,128)} async-done(((f32[2,1024,1024]{2,1,0:T(8,128)}), f32[2,1024,512]{2,1,0:T(8,128)}) %reduce-scatter.5.cloned.1.call-update) | async-done | bytes 4194320 | tf_op jit(solution)/shard_map/reduce_scatter | solution.py:40
  115.5 0.0 reduce-scatter.7.cloned.1.call-update
  115.5 0.0 all-gather.7.cloned.1.call-start
  115.6 0.1 compare_convert_fusion
  115.6 74.7 %reduce-scatter.7.cloned.1.call-done = f32[2,64,512]{2,1,0:T(8,128)} async-done(((f32[2,1024,512]{2,1,0:T(8,128)}), f32[2,64,512]{2,1,0:T(8,128)}) %reduce-scatter.7.cloned.1.call-update) | async-done | bytes 262160 | tf_op jit(solution)/shard_map/reduce_scatter | solution.py:41
  190.4 1.0 multiply_add_fusion
  191.4 6.5 all_gather.33
  197.9 0.1 abs_reduce_fusion
  198.0 0.1 reduce_max.9
  198.1 22.6 %pmax.7 = f32[2]{0:T(128)S(1)} all-reduce(f32[2]{0:T(128)S(1)} %reduce_max.9), channel_id=1, replica_groups=mesh['dp'=16,'grp'=2] {'dp'}, use_global_device_ids=true, to_apply=%region_4.0 | all-reduce | flops 2 | bytes 16 | tf_op jit(solution)/shard_map/pmax | solution.py:50
  220.7 0.8 broadcast_multiply_fusion
  221.5 0.0 all-gather.7.cloned.1.call-update
  221.5 0.0 all-gather.9.cloned.1.call-start
  221.6 56.9 %all-gather.7.cloned.1.call-done = f32[2,1024,512]{2,1,0:T(8,128)} async-done(((f32[2,64,512]{2,1,0:T(8,128)}), f32[2,1024,512]{2,1,0:T(8,128)}) %all-gather.7.cloned.1.call-update) | async-done | bytes 4194320 | tf_op jit(solution)/shard_map/all_gather | solution.py:54
  278.5 5.0 fusion.2
  283.5 8.3 %all_gather.35 = f32[2,64,1024]{2,1,0:T(8,128)S(1)} all-gather(f32[2,64,512]{2,1,0:T(8,128)S(1)} %fusion.2), channel_id=1, replica_groups=mesh['dp'=16,'grp'=2] {'grp'}, dimensions={2}, use_global_device_ids=true | all-gather | bytes 786432 | tf_op jit(solution)/shard_map/all_gather | solution.py:56
  291.7 3.4 convolution_subtract_fusion.3
  295.1 0.0 all-gather.9.cloned.1.call-update
  295.1 0.0 all-gather.11.cloned.1.call-start
  295.2 49.9 %all-gather.9.cloned.1.call-done = f32[2,1024,512]{2,1,0:T(8,128)} async-done(((f32[2,64,512]{2,1,0:T(8,128)}), f32[2,1024,512]{2,1,0:T(8,128)}) %all-gather.9.cloned.1.call-update) | async-done | bytes 4194320 | tf_op jit(solution)/shard_map/all_gather | solution.py:54
  345.0 5.0 fusion.3
  350.0 8.4 %all_gather.37 = f32[2,64,1024]{2,1,0:T(8,128)S(1)} all-gather(f32[2,64,512]{2,1,0:T(8,128)S(1)} %fusion.3), channel_id=1, replica_groups=mesh['dp'=16,'grp'=2] {'grp'}, dimensions={2}, use_global_device_ids=true | all-gather | bytes 786432 | tf_op jit(solution)/shard_map/all_gather | solution.py:56
  358.5 3.4 convolution_subtract_fusion.2
  361.9 0.0 all-gather.13.cloned.1.call-start
  361.9 49.9 %all-gather.11.cloned.1.call-done = f32[2,1024,512]{2,1,0:T(8,128)} async-done(((f32[2,64,512]{2,1,0:T(8,128)}), f32[2,1024,512]{2,1,0:T(8,128)}) %all-gather.11.cloned.1.call-update) | async-done | bytes 4194320 | tf_op jit(solution)/shard_map/all_gather | solution.py:54
  411.8 5.0 fusion.4
  416.8 8.3 %all_gather.39 = f32[2,64,1024]{2,1,0:T(8,128)S(1)} all-gather(f32[2,64,512]{2,1,0:T(8,128)S(1)} %fusion.4), channel_id=1, replica_groups=mesh['dp'=16,'grp'=2] {'grp'}, dimensions={2}, use_global_device_ids=true | all-gather | bytes 786432 | tf_op jit(solution)/shard_map/all_gather | solution.py:56
  425.0 3.3 convolution_subtract_fusion.1
  428.4 0.0 all-gather.15.cloned.1.call-start
  428.4 49.9 %all-gather.13.cloned.1.call-done = f32[2,1024,512]{2,1,0:T(8,128)} async-done(((f32[2,64,512]{2,1,0:T(8,128)}), f32[2,1024,512]{2,1,0:T(8,128)}) %all-gather.13.cloned.1.call-update) | async-done | bytes 4194320 | tf_op jit(solution)/shard_map/all_gather | solution.py:54
  478.4 5.0 fusion.5
  483.3 8.3 %all_gather.41 = f32[2,64,1024]{2,1,0:T(8,128)S(1)} all-gather(f32[2,64,512]{2,1,0:T(8,128)S(1)} %fusion.5), channel_id=1, replica_groups=mesh['dp'=16,'grp'=2] {'grp'}, dimensions={2}, use_global_device_ids=true | all-gather | bytes 786432 | tf_op jit(solution)/shard_map/all_gather | solution.py:56
  491.6 3.3 convolution_subtract_fusion
  495.0 0.0 all-gather.17.cloned.1.call-start
  495.0 49.9 %all-gather.15.cloned.1.call-done = f32[2,1024,512]{2,1,0:T(8,128)} async-done(((f32[2,64,512]{2,1,0:T(8,128)}), f32[2,1024,512]{2,1,0:T(8,128)}) %all-gather.15.cloned.1.call-update) | async-done | bytes 4194320 | tf_op jit(solution)/shard_map/all_gather | solution.py:59
  544.9 0.3 reduce-scatter.9.cloned.1.call-start
  545.2 104.1 %all-gather.17.cloned.1.call-done = f32[2,1024,1024]{2,1,0:T(8,128)} async-done(((f32[2,1024,512]{2,1,0:T(8,128)}), f32[2,1024,1024]{2,1,0:T(8,128)}) %all-gather.17.cloned.1.call-update) | async-done | bytes 8388624 | tf_op jit(solution)/shard_map/all_gather | solution.py:60
  649.3 8.6 %fusion.1 = f32[1024,512]{1,0:T(8,128)S(1)} fusion(bf16[512,1024]{1,0:T(8,128)(2,1)S(1)} %copy-done, f32[2,1024,1024]{2,1,0:T(8,128)} %all-gather.17.cloned.1.call-done), kind=kOutput, calls=%fused_computation.4 | convolution fusion | flops 6442450944 | bytes 7340032 | tf_op jit(solution)/shard_map/dot_general | solution.py:61
  657.9 8.6 %fusion = f32[1024,512]{1,0:T(8,128)S(1)} fusion(bf16[512,1024]{1,0:T(8,128)(2,1)S(1)} %copy-done.8, f32[2,1024,1024]{2,1,0:T(8,128)} %all-gather.17.cloned.1.call-done), kind=kOutput, calls=%fused_computation.2 | convolution fusion | flops 6442450944 | bytes 7340032 | tf_op jit(solution)/shard_map/dot_general | solution.py:62
  666.5 8.3 %convolution_multiply_fusion = f32[1024,1024]{1,0:T(8,128)} fusion(f32[1024,512]{1,0:T(8,128)S(1)} %fusion.1, f32[1024,512]{1,0:T(8,128)S(1)} %fusion), kind=kOutput, calls=%fused_computation.5 | convolution fusion | flops 6443499520 | bytes 8388608 | tf_op jit(solution)/shard_map/dot_general | solution.py:64
  674.8 0.0 reduce-scatter.11.cloned.1.call-start
  674.9 71.1 %reduce-scatter.9.cloned.1.call-done = f32[64,1024]{1,0:T(8,128)} async-done(((f32[1024,1024]{1,0:T(8,128)}), f32[64,1024]{1,0:T(8,128)}) %reduce-scatter.9.cloned.1.call-update) | async-done | bytes 262160 | tf_op jit(solution)/shard_map/reduce_scatter | solution.py:63
  746.0 14.7 %reduce-scatter.11.cloned.1.call-done = f32[64,512]{1,0:T(8,128)} async-done(((f32[64,1024]{1,0:T(8,128)}), f32[64,512]{1,0:T(8,128)}) %reduce-scatter.11.cloned.1.call-update) | async-done | bytes 131088 | tf_op jit(solution)/shard_map/reduce_scatter | solution.py:72
  (30 shorter events, 0.2 us)
Async XLA Ops:
  6.5 3.0 copy-start
  6.5 108.9 %reduce-scatter.5.cloned.1.call-start = ((), (), s32[]{:S(2)}) async-start(), calls=%async_computation.4 | async-start | bytes 12582912 | tf_op jit(solution)/shard_map/reduce_scatter | solution.py:40
  15.0 175.3 %copy-start.9 = (f32[2]{0:T(128)S(1)}, f32[2]{0:T(128)}, u32[]{:S(2)}) copy-start(f32[2]{0:T(128)} %param.5) | copy-start | bytes 28
  15.1 175.3 %reduce-scatter.7.cloned.1.call-start = ((), (), s32[]{:S(2)}) async-start(), calls=%async_computation.5 | async-start | bytes 4456448 | tf_op jit(solution)/shard_map/reduce_scatter | solution.py:41
  115.5 163.0 %all-gather.7.cloned.1.call-start = ((), (), s32[]{:S(2)}) async-start(), calls=%async_computation.6 | async-start | bytes 4456448 | tf_op jit(solution)/shard_map/all_gather | solution.py:54
  221.5 123.5 %all-gather.9.cloned.1.call-start = ((), (), s32[]{:S(2)}) async-start(), calls=%async_computation.7 | async-start | bytes 4456448 | tf_op jit(solution)/shard_map/all_gather | solution.py:54
  278.5 13.3 %copy-start.4 = (f32[2,1024,512]{2,1,0:T(8,128)S(1)}, f32[2,1024,512]{2,1,0:T(8,128)}, u32[]{:S(2)}) copy-start(f32[2,1024,512]{2,1,0:T(8,128)} %all-gather.7.cloned.1.call-done) | copy-start | bytes 12582916
  295.1 63.4 %copy-start.7 = (f32[2,64,512]{2,1,0:T(8,128)S(1)}, f32[2,64,512]{2,1,0:T(8,128)}, u32[]{:S(2)}) copy-start(f32[2,64,512]{2,1,0:T(8,128)} %convolution_subtract_fusion.3) | copy-start | bytes 786436
  295.1 116.7 %all-gather.11.cloned.1.call-start = ((), (), s32[]{:S(2)}) async-start(), calls=%async_computation.8 | async-start | bytes 4456448 | tf_op jit(solution)/shard_map/all_gather | solution.py:54
  345.0 13.4 %copy-start.2 = (f32[2,1024,512]{2,1,0:T(8,128)S(1)}, f32[2,1024,512]{2,1,0:T(8,128)}, u32[]{:S(2)}) copy-start(f32[2,1024,512]{2,1,0:T(8,128)} %all-gather.9.cloned.1.call-done) | copy-start | bytes 12582916
  361.8 63.2 %copy-start.6 = (f32[2,64,512]{2,1,0:T(8,128)S(1)}, f32[2,64,512]{2,1,0:T(8,128)}, u32[]{:S(2)}) copy-start(f32[2,64,512]{2,1,0:T(8,128)} %convolution_subtract_fusion.2) | copy-start | bytes 786436
  361.9 116.5 %all-gather.13.cloned.1.call-start = ((), (), s32[]{:S(2)}) async-start(), calls=%async_computation.9 | async-start | bytes 4456448 | tf_op jit(solution)/shard_map/all_gather | solution.py:54
  411.8 13.3 %copy-start.3 = (f32[2,1024,512]{2,1,0:T(8,128)S(1)}, f32[2,1024,512]{2,1,0:T(8,128)}, u32[]{:S(2)}) copy-start(f32[2,1024,512]{2,1,0:T(8,128)} %all-gather.11.cloned.1.call-done) | copy-start | bytes 12582916
  428.4 63.2 %copy-start.5 = (f32[2,64,512]{2,1,0:T(8,128)S(1)}, f32[2,64,512]{2,1,0:T(8,128)}, u32[]{:S(2)}) copy-start(f32[2,64,512]{2,1,0:T(8,128)} %convolution_subtract_fusion.1) | copy-start | bytes 786436
  428.4 116.5 %all-gather.15.cloned.1.call-start = ((), (), s32[]{:S(2)}) async-start(), calls=%async_computation.10 | async-start | bytes 4456448 | tf_op jit(solution)/shard_map/all_gather | solution.py:59
  478.4 13.3 %copy-start.1 = (f32[2,1024,512]{2,1,0:T(8,128)S(1)}, f32[2,1024,512]{2,1,0:T(8,128)}, u32[]{:S(2)}) copy-start(f32[2,1024,512]{2,1,0:T(8,128)} %all-gather.13.cloned.1.call-done) | copy-start | bytes 12582916
  495.0 154.3 %all-gather.17.cloned.1.call-start = ((), (), s32[]{:S(2)}) async-start(), calls=%async_computation.11 | async-start | bytes 12582912 | tf_op jit(solution)/shard_map/all_gather | solution.py:60
  544.9 112.9 %copy-start.8 = (bf16[512,1024]{1,0:T(8,128)(2,1)S(1)}, bf16[512,1024]{1,0:T(8,128)(2,1)}, u32[]{:S(2)}) copy-start(bf16[512,1024]{1,0:T(8,128)(2,1)} %param.4) | copy-start | bytes 3145732
  544.9 201.0 %reduce-scatter.9.cloned.1.call-start = ((), (), s32[]{:S(2)}) async-start(), calls=%async_computation.12 | async-start | bytes 4456448 | tf_op jit(solution)/shard_map/reduce_scatter | solution.py:63
  674.8 85.8 %reduce-scatter.11.cloned.1.call-start = ((), (), s32[]{:S(2)}) async-start(), calls=%async_computation.13 | async-start | bytes 393216 | tf_op jit(solution)/shard_map/reduce_scatter | solution.py:72
Sparse Core Ops, SparseCore 0:
  15.2 100.2 reduce-scatter.4
  119.3 70.9 reduce-scatter.6
  221.6 56.7 all-gather.6
  295.2 49.7 all-gather.8
  362.0 49.7 all-gather.10
  428.5 49.7 all-gather.12
  495.1 49.7 all-gather.14
  546.4 102.7 all-gather.16
  674.9 70.9 reduce-scatter.8
  748.0 12.5 reduce-scatter.10
where the time goes:
time: 769 us; the launch traced here: 767 us
  waiting for transfers between devices  621 us (81%)
  matrix products  63.1 us (8%)
  blocking collectives  62.2 us (8%)
  between operations  13.6 us (2%)
    all_gather x4, waiting for transfers between devices, local(): columns = lax.all_gather(iterate, 'dp', axis=1, tiled=True)  207 us
    all_gather x1, waiting for transfers between devices, local(): inverses = lax.all_gather(inverse_cols, 'grp', axis=2, tiled=True)  104 us
    reduce_scatter x1, waiting for transfers between devices, local(): lax.psum_scatter(stacked, 'grp', scatter_dimension=2, tiled=True)  100 us
    reduce_scatter x1, waiting for transfers between devices, local(): block = lax.psum_scatter(column_sums, 'dp', scatter_dimension=1, tiled=True)  74.7 us
    reduce_scatter x1, waiting for transfers between devices, local(): lax.psum_scatter(lax.dot_general(mapped, weighted, contract, precision=hi...  71.1 us
    all_gather x1, waiting for transfers between devices, local(): inverse_cols = lax.all_gather(iterate, 'dp', axis=1, tiled=True)  49.9 us
    dot_general x8, matrix products, batched(): jnp.einsum('bij,bjk->bik', left, right, precision=lax.Precision.HIGHEST,...  33.4 us
    all_gather x4, blocking collectives, local(): image_rows = lax.all_gather(image, 'grp', axis=2, tiled=True)  33.2 us
  transfers between devices with their start and end apart: 10, of which 10 were waited for; matrix products, arithmetic and copies ran while one was open for 0% of the time, Pallas kernels for 0%

commit v1 on v0

v1 whole, which is shorter than its diff:
```python
import jax
import jax.numpy as jnp
from jax import lax
from jax.sharding import PartitionSpec as P


def product(left, right):
    return jnp.dot(left, right, precision=lax.Precision.HIGH, preferred_element_type=jnp.float32)


def factors(matrix):
    alpha = 1.0 / jnp.max(jnp.sum(jnp.abs(matrix), axis=1))
    first = jnp.eye(matrix.shape[0], dtype=jnp.float32) - alpha * matrix
    second = product(first, first)
    return alpha, first, second, product(second, second)


def apply_inverse(block, parts):
    alpha, first, second, fourth = parts
    block = block + product(block, first)
    block = block + product(block, second)
    block = block + product(block, fourth)
    return alpha * (block + product(product(block, fourth), fourth))


def local(acts, grads, damping):
    dp_size = lax.axis_size("dp")
    grp_size = lax.axis_size("grp")
    width = acts.shape[1]
    scale = 1.0 / (acts.shape[0] * dp_size * grp_size)
    contract = (((0,), (0,)), ((), ()))

    def gram(left, right):
        return lax.dot_general(left, right, contract, preferred_element_type=jnp.float32) * scale

    terms = jnp.stack([gram(acts, acts), gram(grads, grads), gram(grads, acts)])
    rows = lax.psum_scatter(terms, "dp", scatter_dimension=1, tiled=True)
    rows = lax.psum_scatter(rows, "grp", scatter_dimension=1, tiled=True)
    grams = lax.all_gather(rows[:2], ("dp", "grp"), axis=1, tiled=True)
    eye = jnp.eye(width, dtype=jnp.float32)
    left = factors(grams[0] + damping[0] * eye)
    right = factors(grams[1] + damping[1] * eye)
    mapped = apply_inverse(rows[2], left).T
    mapped = lax.all_to_all(mapped, ("dp", "grp"), 0, 1, tiled=True)
    result = apply_inverse(mapped, right)
    return lax.all_to_all(result, "grp", 1, 0, tiled=True)


def solution(mesh):
    placed = (P(("dp", "grp"), None), P(("dp", "grp"), None), P())
    return jax.shard_map(
        local, mesh=mesh, in_specs=placed, out_specs=P("dp", "grp"), check_vma=False
    )
```

time: 769 us -> 351 us (0.46)
  the two profiles are of different devices: /device:TPU:13 before, /device:TPU:0 now
where the time goes in v1:
time: 351 us; the launch traced here: 345 us
  waiting for transfers between devices  235 us (67%)
  matrix products  63.6 us (18%)
  between operations  15.1 us (4%)
  other arithmetic  12.5 us (4%)
  local copies, waits for them, and re-layouts  8.36 us (2%)
  blocking collectives  7.31 us (2%)
    reduce_scatter x1, waiting for transfers between devices, local(): rows = lax.psum_scatter(terms, 'dp', scatter_dimension=1, tiled=True)  138 us
    all_gather x1, waiting for transfers between devices, local(): grams = lax.all_gather(rows[:2], ('dp', 'grp'), axis=1, tiled=True)  78 us
    dot_general x14, matrix products, product(): jnp.dot(left, right, precision=lax.Precision.HIGH, preferred_element_type...  59.8 us
    reduce_scatter x1, waiting for transfers between devices, local(): rows = lax.psum_scatter(rows, 'grp', scatter_dimension=1, tiled=True)  19 us
    all_to_all x1, blocking collectives, local(): return lax.all_to_all(result, 'grp', 1, 0, tiled=True)  7.31 us
  transfers between devices with their start and end apart: 4, of which 3 were waited for; matrix products, arithmetic and copies ran while one was open for 6% of the time, Pallas kernels for 0%

profile of v1, /device:TPU:0, one launch (start us, length us, event | category | flops | bytes accessed | tf_op | source)
XLA Modules:
  0.0 344.7 jit_solution(6166863990974076301)
XLA Ops:
  6.5 0.0 copy-start
  6.5 0.0 reduce-scatter.3.cloned.1.call-start
  6.5 1.2 copy-done
  7.8 1.3 multiply_bitcast_fusion.1
  9.0 0.0 copy-done.5
  9.1 1.3 multiply_bitcast_fusion
  10.4 1.3 multiply_bitcast_fusion.2
  11.7 4.8 %pad_maximum_fusion = f32[3,1024,1024]{2,1,0:T(8,128)} fusion(f32[1,1024,1024]{2,1,0:T(8,128)S(1)} %multiply_bitcast_fusion, f32[1,1024,1024]{2,1,0:T(8,128)S(1)} %multiply_bitcast_fusion.1, f32[1,1024,1024]{2,1,0:T(8,128)S(1)} %multiply_bitcast_fusion.2), kind=kLoop, calls=%fused_computation | loop fusion | flops 6291456 | bytes 25165824 | tf_op jit(solution)/shard_map/stack | solution.py:36
  16.5 0.0 reduce-scatter.3.cloned.1.call-update
  16.5 0.0 reduce-scatter.5.cloned.1.call-start
  16.6 137.6 %reduce-scatter.3.cloned.1.call-done = f32[3,64,1024]{2,1,0:T(8,128)} async-done(((f32[3,1024,1024]{2,1,0:T(8,128)}), f32[3,64,1024]{2,1,0:T(8,128)}) %reduce-scatter.3.cloned.1.call-update) | async-done | bytes 786448 | tf_op jit(solution)/shard_map/reduce_scatter | solution.py:37
  154.2 0.0 reduce-scatter.5.cloned.1.call-update
  154.2 0.0 all-gather.2.cloned.1.call-start
  154.2 19.0 %reduce-scatter.5.cloned.1.call-done = f32[3,32,1024]{2,1,0:T(8,128)} async-done(((f32[3,64,1024]{2,1,0:T(8,128)}), f32[3,32,1024]{2,1,0:T(8,128)}) %reduce-scatter.5.cloned.1.call-update) | async-done | bytes 393232 | tf_op jit(solution)/shard_map/reduce_scatter | solution.py:38
  173.2 1.7 slice.24
  174.9 0.0 all-gather.2.cloned.1.call-update
  174.9 0.6 fusion.39
  175.5 78.0 %all-gather.2.cloned.1.call-done = f32[2,1024,1024]{2,1,0:T(8,128)} async-done(((f32[2,32,1024]{2,1,0:T(8,128)}), f32[2,1024,1024]{2,1,0:T(8,128)}) %all-gather.2.cloned.1.call-update) | async-done | bytes 8388624 | tf_op jit(solution)/shard_map/all_gather | solution.py:39
  253.5 5.5 %fusion.5 = (f32[1024]{0:T(1024)S(1)}, f32[1024]{0:T(1024)S(1)}) fusion(f32[2,1024,1024]{2,1,0:T(8,128)} %all-gather.2.cloned.1.call-done, f32[]{:T(128)} %bitcast.4, f32[]{:T(128)} %bitcast.6), kind=kLoop, calls=%fused_computation.10 | loop fusion | flops 9435136 | bytes 8396808 | tf_op jit(solution)/shard_map/reduce_sum | solution.py:12
  258.9 0.6 reduce_max.19
  260.2 11.8 %fusion.10 = f32[1024,1024]{1,0:T(8,128)S(1)} fusion(f32[2,1024,1024]{2,1,0:T(8,128)} %all-gather.2.cloned.1.call-done, f32[]{:T(128)} %bitcast.6, f32[]{:T(128)S(6)} %div.7), kind=kOutput, calls=%fused_computation.18 | convolution fusion | flops 6448742400 | bytes 8389124 | tf_op jit(solution)/shard_map/dot_general | solution.py:8
  272.0 6.7 %fusion.40 = f32[1024,1024]{1,0:T(8,128)S(1)} fusion(f32[1024,1024]{1,0:T(8,128)S(1)} %fusion.10), kind=kOutput, calls=%fused_computation.51 | convolution fusion | flops 6442450944 | bytes 8388608 | tf_op jit(solution)/shard_map/dot_general | solution.py:8
  278.8 3.1 fusion.26
  281.9 1.3 convolution_add_fusion.3
  283.3 1.3 convolution_add_fusion.2
  284.6 1.3 fusion.41
  285.9 1.6 fusion.31
  287.5 0.2 all_to_all.28
  287.7 0.3 copy.14
  288.0 0.9 reshape.42
  288.9 3.2 all-to-all-start
  292.1 0.6 reduce_max.18
  293.3 11.5 %fusion.6 = f32[1024,1024]{1,0:T(8,128)S(1)} fusion(f32[2,1024,1024]{2,1,0:T(8,128)} %all-gather.2.cloned.1.call-done, f32[]{:T(128)} %bitcast.4, f32[]{:T(128)S(6)} %div.6), kind=kOutput, calls=%fused_computation.16 | convolution fusion | flops 6448742400 | bytes 8389124 | tf_op jit(solution)/shard_map/dot_general | solution.py:8
  304.8 2.0 copy-done.3
  306.8 8.5 %fusion.42 = f32[1024,1024]{1,0:T(8,128)} fusion(f32[1024,1024]{1,0:T(8,128)S(1)} %fusion.6), kind=kOutput, calls=%fused_computation.53 | convolution fusion | flops 6442450944 | bytes 8388608 | tf_op jit(solution)/shard_map/dot_general | solution.py:8
  315.2 0.0 all-to-all-done
  315.3 0.5 broadcast.79
  315.8 0.9 reduce
  316.7 0.2 reshape.43
  316.9 0.2 copy.9
  317.1 4.7 %fusion.32 = f32[32,1024]{1,0:T(8,128)S(1)} fusion(f32[32,1024]{1,0:T(8,128)S(1)} %copy.9, f32[32,1024]{0,1:T(8,128)S(1)} %bitcast.81, f32[2,1024,1024]{2,1,0:T(8,128)} %all-gather.2.cloned.1.call-done, f32[]{:T(128)} %bitcast.4, f32[]{:T(128)S(6)} %div.6), kind=kOutput, calls=%fused_computation.42 | convolution fusion | flops 207650816 | bytes 4588036 | tf_op jit(solution)/shard_map/dot_general | solution.py:8
  321.7 3.5 %convolution_add_fusion.1 = f32[32,1024]{1,0:T(8,128)S(1)} fusion(f32[32,1024]{1,0:T(8,128)S(1)} %fusion.32, f32[1024,1024]{1,0:T(8,128)} %copy-done.3), kind=kOutput, calls=%fused_computation.33 | convolution fusion | flops 201359360 | bytes 4456448 | tf_op jit(solution)/shard_map/dot_general | solution.py:8
  325.3 0.0 copy-done.1
  325.3 1.5 convolution_add_fusion
  326.8 1.5 fusion.43
  328.2 1.5 fusion.29
  329.7 7.3 %all_to_all.38 = f32[32,2,512]{2,0,1:T(8,128)S(1)} all-to-all(f32[32,2,512]{2,0,1:T(8,128)S(1)} %bitcast.84), channel_id=1, replica_groups=mesh['dp'=16,'grp'=2] {'grp'}, dimensions={1} | all-to-all | bytes 262144 | tf_op jit(solution)/shard_map/all_to_all | solution.py:46
  337.0 0.7 copy.16
  (8 shorter events, 0.0 us)
Async XLA Ops:
  6.5 1.2 copy-start
  6.5 2.5 copy-start.5
  6.5 147.6 %reduce-scatter.3.cloned.1.call-start = ((), (), s32[]{:S(2)}) async-start(), calls=%async_computation.4 | async-start | bytes 13369344 | tf_op jit(solution)/shard_map/reduce_scatter | solution.py:37
  16.5 158.4 %copy-start.4 = (f32[2]{0:T(128)S(1)}, f32[2]{0:T(128)}, u32[]{:S(2)}) copy-start(f32[2]{0:T(128)} %param.5) | copy-start | bytes 28
  16.5 156.7 %reduce-scatter.5.cloned.1.call-start = ((), (), s32[]{:S(2)}) async-start(), calls=%async_computation.5 | async-start | bytes 1179648 | tf_op jit(solution)/shard_map/reduce_scatter | solution.py:38
  154.2 99.3 %all-gather.2.cloned.1.call-start = ((), (), s32[]{:S(2)}) async-start(), calls=%async_computation.6 | async-start | bytes 8650752 | tf_op jit(solution)/shard_map/all_gather | solution.py:39
  272.0 6.8 %copy-start.2 = (f32[2,1024,1024]{2,1,0:T(8,128)S(1)}, f32[2,1024,1024]{2,1,0:T(8,128)}, u32[]{:S(2)}) copy-start(f32[2,1024,1024]{2,1,0:T(8,128)} %all-gather.2.cloned.1.call-done) | copy-start | bytes 25165828
  288.9 26.4 %all-to-all-start = ((f32[32,1,1024]{2,1,0:T(1,128)}), f32[32,1,1024]{2,1,0:T(1,128)S(1)}, u32[]{:S(2)}, u32[]{:S(2)}) async-start(f32[32,1,1024]{2,1,0:T(1,128)} %reshape.42), calls=%async_computation.2 | async-start | bytes 262144 | tf_op jit(solution)/shard_map/all_to_all | solution.py:44
  304.8 2.0 copy-start.3
  317.1 8.2 %copy-start.1 = (f32[1024,1024]{1,0:T(8,128)S(1)}, f32[1024,1024]{1,0:T(8,128)}, u32[]{:S(2)}) copy-start(f32[1024,1024]{1,0:T(8,128)} %fusion.42) | copy-start | bytes 12582916
Sparse Core Ops, SparseCore 0:
  16.6 137.4 reduce-scatter.2
  156.4 16.7 reduce-scatter.4
  176.2 77.2 all-gather.1
